TPU v7x, 32 devices: a whole 2x2x4 slice. The times are simulated.
32 devices in a mesh: survey: 2 (over y), off: 8 (over z, x), gy: 2 (over core).
Axes of the slice: x: 2, y: 2, z: 4, core: 2. Of those that a mesh axis runs over, the one named last changes fastest.
Arguments:
- checkpoint: float32 [16, 2, 2, 16, 48, 256], P(('survey', 'off'), None, None, 'gy'), parts along dimension 0, may hold values from -6 to 6
- traces: float32 [16, 4, 16, 256], P(('survey', 'off'), None, 'gy'), parts along dimension 0, may hold values from -6 to 6
- courant_sq: float32 [16, 48, 256], P('gy'), may hold values from 0.06 to 0.18
- holder: int32 [8], P('survey'), parts along dimension 0, may hold values from 0 to 7, as said below
- offset_lags: int32 [16, 4], P(('survey', 'off')), parts along dimension 0, may hold values from -16 to 15, as said below
Outputs:
- offset_image: float32 [64, 16, 48, 256], P(('survey', 'off'), 'gy'), parts along dimension 0
There are 2 independent parts, one for each index of `survey`. A program takes and returns all parts, laid end to end along the dimension named above; an argument that names none is the same for every part. Nothing has to cross between parts.
Inputs may be any that keep to these rules, and one draw needn't show every extreme that they name: `holder`: the 4 entries are distinct; every draw contains both 0 and 8 - 1. `offset_lags`: each of the 32 values from -16 to 15 appears exactly once.
All inputs are finite; a program needn't handle non-finite values.
Results may differ from a plain program's by a relative error of at most 0.0041.
Values may be sent and summed in bfloat16 or wider, within the bound.
No kernel may reach another device: no remote copies, remote signals or barrier semaphores. Data moves between devices by JAX's collectives and lax.ppermute only.
A program may use at most 128 MiB of HBM per device.

v0:
```python
import jax
import jax.numpy as jnp
from jax import lax
from jax.sharding import PartitionSpec as P

stencil_taps = (-205.0 / 72.0, 8.0 / 5.0, -1.0 / 5.0, 8.0 / 315.0, -1.0 / 560.0)


def extended_2(shard, sides, width):
    for axis, dim in sides:
        devices, length = (lax.axis_size(axis), shard.shape[dim])
        up = [(i, (i + 1) % devices) for i in range(devices - 1)]
        down = [(j, i) for i, j in up]
        last = lax.slice_in_dim(shard, length - width, length, axis=dim)
        initial = lax.slice_in_dim(shard, 0, width, axis=dim)
        before = lax.ppermute(last, axis, up)
        after = lax.ppermute(initial, axis, down)
        shard = jnp.concatenate([before, shard, after], axis=dim)
    return shard


def spread(value, axis, source):
    kept = jnp.where(lax.axis_index(axis) == source, value, 0).astype(value.dtype)
    return lax.psum(kept, axis)


def laplace(extended):
    cells_y = extended.shape[-3] - 8
    cells_z = extended.shape[-2]
    cells_x = extended.shape[-1]
    leading = [(0, 0)] * (extended.ndim - 2)
    padded = jnp.pad(extended, leading + [(4, 4), (4, 4)])

    def shifted(step_y, step_z, step_x):
        return padded[
            ...,
            4 + step_y : 4 + step_y + cells_y,
            4 + step_z : 4 + step_z + cells_z,
            4 + step_x : 4 + step_x + cells_x,
        ]

    summed = 3.0 * stencil_taps[0] * shifted(0, 0, 0)
    for tap_no in range(1, 5):
        beside_all = shifted(tap_no, 0, 0) + shifted(-tap_no, 0, 0)
        beside_all = beside_all + shifted(0, tap_no, 0) + shifted(0, -tap_no, 0)
        beside_all = beside_all + shifted(0, 0, tap_no) + shifted(0, 0, -tap_no)
        summed = summed + stencil_taps[tap_no] * beside_all
    return summed


def propagate_step(earlier, current, courant_sq, drive):
    extended = extended_2(current, (("gy", 2),), 4)
    advanced = 2.0 * current - earlier + courant_sq * laplace(extended)
    advanced = advanced.at[:, 1, :, 0, :].add(drive)
    return (current, advanced)


def correlate(image_acc, source, receiver, my_lags, half_span):
    cells_x = receiver.shape[-1]
    padded = jnp.pad(receiver, ((0, 0), (0, 0), (half_span, half_span)))
    moved = jax.vmap(
        lambda lag_value: lax.dynamic_slice_in_dim(padded, half_span + lag_value, cells_x, 2)
    )(my_lags)
    return image_acc + source.astype(jnp.float32)[None] * moved.astype(jnp.float32)


def on_device(checkpoint, traces, courant_sq, holder, offset_lags):
    shot_count = holder.shape[0]
    step_count = traces.shape[1]
    my_lags = offset_lags[0]
    half_span = lax.axis_size("off") * offset_lags.shape[1] // 2
    image_acc = jnp.zeros((offset_lags.shape[1],) + courant_sq.shape, jnp.float32)
    earlier = checkpoint[:, 0]
    current = checkpoint[:, 1]
    collected = []
    for step_no in range(step_count):
        earlier, current = propagate_step(earlier, current, courant_sq, traces[:, step_no])
        if step_no % 2 == 1:
            snapshot = current[0].astype(jnp.bfloat16)
            collected.append(snapshot)
    snap_runs = jnp.stack(collected)
    for shot_no in range(shot_count):
        received = spread(snap_runs, "off", holder[shot_no])
        for snap_no in range(received.shape[0]):
            image_acc = correlate(
                image_acc, received[snap_no, 0], received[snap_no, 1], my_lags, half_span
            )
    return image_acc


def solution(mesh):
    placed = (
        P(("survey", "off"), None, None, "gy", None, None),
        P(("survey", "off"), None, "gy", None),
        P("gy", None, None),
        P("survey"),
        P(("survey", "off"), None),
    )
    return jax.shard_map(
        on_device,
        mesh=mesh,
        in_specs=placed,
        out_specs=P(("survey", "off"), "gy", None, None),
        check_vma=False,
    )
```

profile of v0, /device:TPU:0, one launch (start us, length us, event | category | flops | bytes accessed | tf_op | source)
XLA Modules:
  0.0 278.0 jit_solution(1497797159843824747)
XLA Ops:
  6.5 1.5 fusion.146
  8.1 0.5 copy.198
  8.8 2.4 collective-permute-start.1
  11.3 1.3 collective-permute-start
  12.9 0.3 copy.142
  13.1 1.8 collective-permute-done
  15.2 1.5 select_maximum_fusion.6
  16.6 3.6 %fusion.103 = f32[1,2,8,48,256]{4,2,3,1,0:T(8,128)S(1)} fusion(f32[1,2,8,48,256]{4,2,3,1,0:T(8,128)S(1)} %bitcast.98, f32[1,2,4,48,256]{4,2,3,1,0:T(4,128)S(1)} %copy.142, f32[1,2,4,48,256]{4,2,3,1,0:T(4,128)S(1)} %copy.140, f32[1,2,16,56,264]{4,2,3,1,0:T(8,128)S(1)} %select_maximum_fusion.6, f32[1,1,2,8,48,256]{5,4,3,2,1,0:T(8,128)S(1)} %get-tuple-element.57, ...), kind=kLoop, calls=%fused_computation.172 | loop fusion | flops 8060928 | bytes 16121856 | tf_op jit(solution)/shard_map/add | solution.py:53
  20.3 0.7 fusion.144
  21.2 2.1 collective-permute-start.3
  23.3 1.3 collective-permute-start.2
  24.9 2.0 collective-permute-done.2
  27.2 1.5 select_maximum_fusion.4
  28.7 3.6 %fusion.73 = f32[1,2,8,48,256]{4,2,3,1,0:T(8,128)S(1)} fusion(f32[1,2,8,48,256]{4,2,3,1,0:T(8,128)S(1)} %fusion.144, f32[1,2,4,48,256]{4,2,3,1,0:T(4,128)S(1)} %copy.148, f32[1,2,4,48,256]{4,2,3,1,0:T(4,128)S(1)} %copy.146, f32[1,2,16,56,264]{4,2,3,1,0:T(8,128)S(1)} %select_maximum_fusion.4, f32[8,48,256]{2,0,1:T(8,128)S(1)} %copy-done.3, ...), kind=kLoop, calls=%fused_computation.142 | loop fusion | flops 8060928 | bytes 16121856 | tf_op jit(solution)/shard_map/add | solution.py:53
  32.6 2.1 collective-permute-start.5
  34.7 1.5 collective-permute-start.4
  36.5 1.9 collective-permute-done.4
  38.6 1.4 select_maximum_fusion.2
  40.1 3.4 %fusion.43 = f32[1,2,8,48,256]{4,2,3,1,0:T(8,128)S(1)} fusion(f32[1,2,8,48,256]{4,2,3,1,0:T(8,128)S(1)} %fusion.143, f32[1,2,4,48,256]{4,2,3,1,0:T(4,128)S(1)} %copy.154, f32[1,2,4,48,256]{4,2,3,1,0:T(4,128)S(1)} %copy.152, f32[1,2,16,56,264]{4,2,3,1,0:T(8,128)S(1)} %select_maximum_fusion.2, f32[1,2,8,48,256]{4,2,3,1,0:T(8,128)S(1)} %fusion.144, ...), kind=kLoop, calls=%fused_computation.112 | loop fusion | flops 8060928 | bytes 16121856 | tf_op jit(solution)/shard_map/add | solution.py:53
  43.5 0.9 copy-done
  44.6 2.2 collective-permute-start.7
  46.9 1.3 collective-permute-start.6
  48.2 0.7 fusion.151
  52.1 1.4 select_maximum_fusion
  53.5 3.7 %fusion.13 = f32[1,2,8,48,256]{4,2,3,1,0:T(8,128)S(1)} fusion(f32[1,2,8,48,256]{4,2,3,1,0:T(8,128)S(1)} %copy-done.1, f32[1,2,4,48,256]{4,2,3,1,0:T(4,128)S(1)} %copy.160, f32[1,2,4,48,256]{4,2,3,1,0:T(4,128)S(1)} %copy.158, f32[1,2,16,56,264]{4,2,3,1,0:T(8,128)S(1)} %select_maximum_fusion, f32[1,2,8,48,256]{4,2,3,1,0:T(8,128)S(1)} %fusion.143, ...), kind=kLoop, calls=%fused_computation.82 | loop fusion | flops 8060928 | bytes 16121856 | tf_op jit(solution)/shard_map/add | solution.py:53
  57.3 0.7 fusion.141
  58.0 1.8 broadcast_select_fusion.3
  59.9 131.8 %all-reduce.16.cloned.1.call-done = (bf16[2,2,8,48,256]{4,2,3,1,0:T(8,128)(2,1)}, bf16[2,2,8,48,256]{4,2,3,1,0:T(8,128)(2,1)}, bf16[2,2,8,48,256]{4,2,3,1,0:T(8,128)(2,1)}, bf16[2,2,8,48,256]{4,2,3,1,0:T(8,128)(2,1)}) async-done(((bf16[2,2,8,48,256]{4,2,3,1,0:T(8,128)(2,1)}, bf16[2,2,8,48,256]{4,2,3,1,0:T(8,128)(2,1)}, bf16[2,2,8,48,256]{4,2,3,1,0:T(8,128)(2,1)}, bf16[2,2,8,48,256]{4,2,3,1,0:T(8,128)(2,1)}), ...) | async-done | bytes 3145744 | tf_op jit(solution)/shard_map/psum | solution.py:24
  191.7 2.4 fusion.133
  194.1 0.4 copy.189
  194.5 0.4 copy.188
  194.9 0.9 pad.66.clone
  195.8 0.9 pad.65.clone
  196.7 0.4 copy.186
  197.1 0.9 pad.63.clone
  198.0 0.4 copy.187
  198.4 0.9 pad.64.clone
  199.3 0.5 copy.175
  199.8 0.5 copy.177
  200.3 1.4 copy.173
  201.7 1.4 copy.171
  203.0 3.2 %gather_fusion.5 = bf16[4,8,48,256]{2,1,3,0:T(8,128)(2,1)} fusion(bf16[8,48,288]{1,0,2:T(8,128)(2,1)} %pad.64.clone, s32[4]{0:T(128)S(1)} %shift-left_bitcast_fusion), kind=kCustom, calls=%fused_computation.5 | custom fusion | bytes 1572912 | tf_op jit(solution)/shard_map/vmap()/gather | solution.py:62
  206.3 3.3 %gather_fusion.4 = bf16[4,8,48,256]{2,1,3,0:T(8,128)(2,1)} fusion(bf16[8,48,288]{1,0,2:T(8,128)(2,1)} %pad.63.clone, s32[4]{0:T(128)S(1)} %shift-left_bitcast_fusion), kind=kCustom, calls=%fused_computation.4 | custom fusion | bytes 1572912 | tf_op jit(solution)/shard_map/vmap()/gather | solution.py:62
  209.6 3.3 %gather_fusion.6 = bf16[4,8,48,256]{2,1,3,0:T(8,128)(2,1)} fusion(bf16[8,48,288]{1,0,2:T(8,128)(2,1)} %pad.65.clone, s32[4]{0:T(128)S(1)} %shift-left_bitcast_fusion), kind=kCustom, calls=%fused_computation.6 | custom fusion | bytes 1572912 | tf_op jit(solution)/shard_map/vmap()/gather | solution.py:62
  212.8 3.2 %gather_fusion.7 = bf16[4,8,48,256]{2,1,3,0:T(8,128)(2,1)} fusion(bf16[8,48,288]{1,0,2:T(8,128)(2,1)} %pad.66.clone, s32[4]{0:T(128)S(1)} %shift-left_bitcast_fusion), kind=kCustom, calls=%fused_computation.7 | custom fusion | bytes 1572912 | tf_op jit(solution)/shard_map/vmap()/gather | solution.py:62
  216.0 2.7 fusion.137
  218.8 2.2 copy.185
  221.0 2.0 pad.62.clone
  222.9 2.2 copy.184
  225.1 2.0 pad.61.clone
  227.1 2.2 copy.182
  229.2 2.0 pad.59.clone
  231.2 2.2 copy.183
  233.3 2.0 pad.60.clone
  235.3 2.3 copy.167
  237.7 2.3 copy.169
  240.0 2.3 copy.165
  242.3 1.5 copy.163
  243.7 3.2 %gather_fusion.1 = bf16[4,8,48,256]{2,1,3,0:T(8,128)(2,1)} fusion(bf16[8,48,288]{1,0,2:T(8,128)(2,1)} %pad.60.clone, s32[4]{0:T(128)S(1)} %shift-left_bitcast_fusion), kind=kCustom, calls=%fused_computation.1 | custom fusion | bytes 1572912 | tf_op jit(solution)/shard_map/vmap()/gather | solution.py:62
  246.9 3.2 %gather_fusion = bf16[4,8,48,256]{2,1,3,0:T(8,128)(2,1)} fusion(bf16[8,48,288]{1,0,2:T(8,128)(2,1)} %pad.59.clone, s32[4]{0:T(128)S(1)} %shift-left_bitcast_fusion), kind=kCustom, calls=%fused_computation | custom fusion | bytes 1572912 | tf_op jit(solution)/shard_map/vmap()/gather | solution.py:62
  250.1 3.2 %gather_fusion.2 = bf16[4,8,48,256]{2,1,3,0:T(8,128)(2,1)} fusion(bf16[8,48,288]{1,0,2:T(8,128)(2,1)} %pad.61.clone, s32[4]{0:T(128)S(1)} %shift-left_bitcast_fusion), kind=kCustom, calls=%fused_computation.2 | custom fusion | bytes 1572912 | tf_op jit(solution)/shard_map/vmap()/gather | solution.py:62
  253.4 3.2 %gather_fusion.3 = bf16[4,8,48,256]{2,1,3,0:T(8,128)(2,1)} fusion(bf16[8,48,288]{1,0,2:T(8,128)(2,1)} %pad.62.clone, s32[4]{0:T(128)S(1)} %shift-left_bitcast_fusion), kind=kCustom, calls=%fused_computation.3 | custom fusion | bytes 1572912 | tf_op jit(solution)/shard_map/vmap()/gather | solution.py:62
  256.5 11.0 %multiply_add_fusion = f32[4,8,48,256]{2,1,3,0:T(8,128)} fusion(bf16[4,8,48,256]{2,1,3,0:T(8,128)(2,1)} %gather_fusion.7, bf16[4,8,48,256]{2,1,3,0:T(8,128)(2,1)} %gather_fusion.6, bf16[4,8,48,256]{2,1,3,0:T(8,128)(2,1)} %gather_fusion.5, bf16[4,8,48,256]{2,1,3,0:T(8,128)(2,1)} %gather_fusion.4, bf16[4,8,48,256]{2,1,3,0:T(8,128)(2,1)} %gather_fusion.3, ...), kind=kLoop, calls=%fused_computation.8 | loop fusion | flops 9043968 | bytes 11010048 | tf_op jit(solution)/shard_map/add | solution.py:64
  267.5 3.7 %copy.179 = f32[4,8,48,256]{3,2,1,0:T(8,128)} copy(f32[4,8,48,256]{2,1,3,0:T(8,128)} %multiply_add_fusion) | data formatting | bytes 3145728 | tf_op jit(solution)/shard_map/add | solution.py:64
  (54 shorter events, 3.4 us)
Async XLA Ops:
  6.5 185.2 %all-reduce.16.cloned.1.call-start = ((), (), s32[]{:S(2)}) async-start(), calls=%async_computation | async-start | bytes 6291456 | tf_op jit(solution)/shard_map/psum | solution.py:24
  8.1 4.8 %copy-start.5 = (f32[1,1,2,8,48,256]{5,4,3,2,1,0:T(8,128)}, f32[1,1,2,8,48,256]{5,4,3,2,1,0:T(8,128)S(1)}, u32[]{:S(2)}) copy-start(f32[1,1,2,8,48,256]{5,4,3,2,1,0:T(8,128)S(1)} %get-tuple-element.58) | copy-start | bytes 2359300
  8.1 4.5 %copy-start.7 = (f32[8,48,256]{2,1,0:T(8,128)S(1)}, f32[8,48,256]{2,1,0:T(8,128)}, u32[]{:S(2)}) copy-start(f32[8,48,256]{2,1,0:T(8,128)} %param.15) | copy-start | bytes 1179652
  8.8 4.1 %collective-permute-start.1 = (f32[1,2,4,48,256]{4,3,2,1,0:T(8,128)S(1)}, f32[1,2,4,48,256]{4,3,2,1,0:T(8,128)S(1)}, u32[]{:S(2)}, u32[]{:S(2)}) collective-permute-start(f32[1,2,4,48,256]{4,3,2,1,0:T(8,128)S(1)} %copy.141), channel_id=1, source_target_pairs={{0,1},{2,3},{4,5},{6,7},{8,9},{10,11},{12,13},{14,15},{16,17},{18,... | collective-permute-start | bytes 1179656 | tf_op jit(solution)/shard_map/ppermute | solution.py:16
  11.3 3.6 %collective-permute-start = (f32[1,2,4,48,256]{4,3,2,1,0:T(8,128)S(1)}, f32[1,2,4,48,256]{4,3,2,1,0:T(8,128)S(1)}, u32[]{:S(2)}, u32[]{:S(2)}) collective-permute-start(f32[1,2,4,48,256]{4,3,2,1,0:T(8,128)S(1)} %copy.139), channel_id=1, source_target_pairs={{1,0},{3,2},{5,4},{7,6},{9,8},{11,10},{13,12},{15,14},{17,16},{19,... | collective-permute-start | bytes 1179656 | tf_op jit(solution)/shard_map/ppermute | solution.py:17
  12.8 3.8 %copy-start.2 = (f32[8,48,256]{2,0,1:T(8,128)}, f32[8,48,256]{2,0,1:T(8,128)S(1)}, u32[]{:S(2)}) copy-start(f32[8,48,256]{2,0,1:T(8,128)S(1)} %copy.138) | copy-start | bytes 1179652
  21.2 3.5 %collective-permute-start.3 = (f32[1,2,4,48,256]{4,3,2,1,0:T(8,128)S(1)}, f32[1,2,4,48,256]{4,3,2,1,0:T(8,128)S(1)}, u32[]{:S(2)}, u32[]{:S(2)}) collective-permute-start(f32[1,2,4,48,256]{4,3,2,1,0:T(8,128)S(1)} %copy.147), channel_id=1, source_target_pairs={{0,1},{2,3},{4,5},{6,7},{8,9},{10,11},{12,13},{14,15},{16,17},{18,... | collective-permute-start | bytes 1179656 | tf_op jit(solution)/shard_map/ppermute | solution.py:16
  23.3 3.6 %collective-permute-start.2 = (f32[1,2,4,48,256]{4,3,2,1,0:T(8,128)S(1)}, f32[1,2,4,48,256]{4,3,2,1,0:T(8,128)S(1)}, u32[]{:S(2)}, u32[]{:S(2)}) collective-permute-start(f32[1,2,4,48,256]{4,3,2,1,0:T(8,128)S(1)} %copy.145), channel_id=1, source_target_pairs={{1,0},{3,2},{5,4},{7,6},{9,8},{11,10},{13,12},{15,14},{17,16},{19,... | collective-permute-start | bytes 1179656 | tf_op jit(solution)/shard_map/ppermute | solution.py:17
  24.9 3.8 %copy-start.3 = (f32[8,48,256]{2,0,1:T(8,128)S(1)}, f32[8,48,256]{2,0,1:T(8,128)}, u32[]{:S(2)}) copy-start(f32[8,48,256]{2,0,1:T(8,128)} %copy-done.2) | copy-start | bytes 1179652
  24.9 3.8 %copy-start.6 = (f32[1,1,2,8,48,256]{5,4,3,2,1,0:T(8,128)S(1)}, f32[1,1,2,8,48,256]{5,4,3,2,1,0:T(8,128)}, u32[]{:S(2)}) copy-start(f32[1,1,2,8,48,256]{5,4,3,2,1,0:T(8,128)} %copy-done.5) | copy-start | bytes 2359300
  28.7 3.7 %copy-start.8 = (f32[1,4,8,256]{3,2,1,0:T(8,128)S(1)}, f32[1,4,8,256]{3,2,1,0:T(8,128)}, u32[]{:S(2)}) copy-start(f32[1,4,8,256]{3,2,1,0:T(8,128)} %param.14) | copy-start | bytes 98308
  32.6 3.6 %collective-permute-start.5 = (f32[1,2,4,48,256]{4,3,2,1,0:T(8,128)S(1)}, f32[1,2,4,48,256]{4,3,2,1,0:T(8,128)S(1)}, u32[]{:S(2)}, u32[]{:S(2)}) collective-permute-start(f32[1,2,4,48,256]{4,3,2,1,0:T(8,128)S(1)} %copy.153), channel_id=1, source_target_pairs={{0,1},{2,3},{4,5},{6,7},{8,9},{10,11},{12,13},{14,15},{16,17},{18,... | collective-permute-start | bytes 1179656 | tf_op jit(solution)/shard_map/ppermute | solution.py:16
  34.7 3.6 %collective-permute-start.4 = (f32[1,2,4,48,256]{4,3,2,1,0:T(8,128)S(1)}, f32[1,2,4,48,256]{4,3,2,1,0:T(8,128)S(1)}, u32[]{:S(2)}, u32[]{:S(2)}) collective-permute-start(f32[1,2,4,48,256]{4,3,2,1,0:T(8,128)S(1)} %copy.151), channel_id=1, source_target_pairs={{1,0},{3,2},{5,4},{7,6},{9,8},{11,10},{13,12},{15,14},{17,16},{19,... | collective-permute-start | bytes 1179656 | tf_op jit(solution)/shard_map/ppermute | solution.py:17
  43.5 4.7 %copy-start.9 = (s32[4]{0:T(128)S(1)}, s32[4]{0:T(128)}, u32[]{:S(2)}) copy-start(s32[4]{0:T(128)} %param.16) | copy-start | bytes 52
  43.5 0.9 copy-start
  44.5 7.5 %copy-start.1 = (f32[1,2,8,48,256]{4,2,3,1,0:T(8,128)S(1)}, f32[1,2,8,48,256]{4,2,3,1,0:T(8,128)}, u32[]{:S(2)}) copy-start(f32[1,2,8,48,256]{4,2,3,1,0:T(8,128)} %copy-done) | copy-start | bytes 2359300
  44.6 6.9 %collective-permute-start.7 = (f32[1,2,4,48,256]{4,3,2,1,0:T(8,128)S(1)}, f32[1,2,4,48,256]{4,3,2,1,0:T(8,128)S(1)}, u32[]{:S(2)}, u32[]{:S(2)}) collective-permute-start(f32[1,2,4,48,256]{4,3,2,1,0:T(8,128)S(1)} %copy.159), channel_id=1, source_target_pairs={{0,1},{2,3},{4,5},{6,7},{8,9},{10,11},{12,13},{14,15},{16,17},{18,... | collective-permute-start | bytes 1179656 | tf_op jit(solution)/shard_map/ppermute | solution.py:16
  46.9 4.9 %collective-permute-start.6 = (f32[1,2,4,48,256]{4,3,2,1,0:T(8,128)S(1)}, f32[1,2,4,48,256]{4,3,2,1,0:T(8,128)S(1)}, u32[]{:S(2)}, u32[]{:S(2)}) collective-permute-start(f32[1,2,4,48,256]{4,3,2,1,0:T(8,128)S(1)} %copy.157), channel_id=1, source_target_pairs={{1,0},{3,2},{5,4},{7,6},{9,8},{11,10},{13,12},{15,14},{17,16},{19,... | collective-permute-start | bytes 1179656 | tf_op jit(solution)/shard_map/ppermute | solution.py:17
  51.8 1.7 copy-start.4
  58.0 1.8 copy-start.10
Sparse Core Ops, SparseCore 0:
  60.0 131.7 all-reduce.15
where the time goes:
time: 279 us; the launch traced here: 278 us
  waiting for transfers between devices  138 us (49%)
  local copies, waits for them, and re-layouts  70.3 us (25%)
  other arithmetic  39.5 us (14%)
  between operations  16.6 us (6%)
  starting transfers between devices  14.1 us (5%)
    psum x1, waiting for transfers between devices, spread(): return lax.psum(kept, axis)  132 us
    gather x8, local copies, waits for them, and re-layouts, correlate(): lax.dynamic_slice_in_dim(padded, half_span + lag_value, cells_x, 2)  25.8 us
    add x4, other arithmetic, propagate_step(): advanced = 2.0 * current - earlier + courant_sq * laplace(extended)  14.4 us
    convert_element_type x8, local copies, waits for them, and re-layouts, correlate(): source.astype(jnp.float32)[None] * moved.astype(jnp.float32)  12.1 us
    unnamed x33, local copies, waits for them, and re-layouts  11.8 us
    pad x8, local copies, waits for them, and re-layouts, correlate(): padded = jnp.pad(receiver, ((0, 0), (0, 0), (half_span, half_span)))  11.6 us
    add x1, other arithmetic, correlate(): image_acc + source.astype(jnp.float32)[None] * moved.astype(jnp.float32)  11 us
    ppermute x4, starting transfers between devices, extended_2(): before = lax.ppermute(last, axis, up)  8.75 us
  transfers between devices with their start and end apart: 9, of which 4 were waited for; matrix products, arithmetic and copies ran while one was open for 1% of the time, Pallas kernels for 0%

commit v1 on v0

--- a/solution.py
+++ b/solution.py
@@ -21,7 +21,7 @@
 
 def spread(value, axis, source):
     kept = jnp.where(lax.axis_index(axis) == source, value, 0).astype(value.dtype)
-    return lax.psum(kept, axis)
+    return jnp.sum(lax.all_gather(kept, axis), axis=0)
 
 
 def laplace(extended):

time: 279 us -> 533 us (1.91)
  waiting for transfers between devices: 138 us -> 389 us
  local copies, waits for them, and re-layouts: 70.3 us -> 58.4 us
  other arithmetic: 39.5 us -> 50.2 us
    all_gather x0 -> x4, waiting for transfers between devices: none -> 384 us  [spread(): return jnp.sum(lax.all_gather(kept, axis), axis=0)]
    psum x1 -> x0, waiting for transfers between devices: 132 us -> none  [spread(): return lax.psum(kept, axis)]
    reduce_sum x0 -> x4, other arithmetic: none -> 15.1 us  [spread(): return jnp.sum(lax.all_gather(kept, axis), axis=0)]
    unnamed x33 -> x34, local copies, waits for them, and re-layouts: 11.8 us -> 3.3 us
    ppermute x4, waiting for transfers between devices: 5.66 us -> 0.01 us  [extended_2(): after = lax.ppermute(initial, axis, down)]
  transfers between devices with their start and end apart: 9 -> 12, of which waited for: 4 -> 7; matrix products, arithmetic and copies ran while one was open for 1% -> 3% of each run, Pallas kernels for 0% -> 0%
where the time goes in v1:
time: 533 us; the launch traced here: 532 us
  waiting for transfers between devices  389 us (73%)
  local copies, waits for them, and re-layouts  58.4 us (11%)
  other arithmetic  50.2 us (9%)
  starting transfers between devices  18 us (3%)
  between operations  16.2 us (3%)
    all_gather x4, waiting for transfers between devices, spread(): return jnp.sum(lax.all_gather(kept, axis), axis=0)  384 us
    gather x8, local copies, waits for them, and re-layouts, correlate(): lax.dynamic_slice_in_dim(padded, half_span + lag_value, cells_x, 2)  26.1 us
    reduce_sum x4, other arithmetic, spread(): return jnp.sum(lax.all_gather(kept, axis), axis=0)  15.1 us
    add x4, other arithmetic, propagate_step(): advanced = 2.0 * current - earlier + courant_sq * laplace(extended)  14.5 us
    ppermute x4, starting transfers between devices, extended_2(): before = lax.ppermute(last, axis, up)  12.3 us
    convert_element_type x8, local copies, waits for them, and re-layouts, correlate(): source.astype(jnp.float32)[None] * moved.astype(jnp.float32)  12.2 us
    add x1, other arithmetic, correlate(): image_acc + source.astype(jnp.float32)[None] * moved.astype(jnp.float32)  11 us
  transfers between devices with their start and end apart: 12, of which 7 were waited for; matrix products, arithmetic and copies ran while one was open for 3% of the time, Pallas kernels for 0%

profile of v1, /device:TPU:0, one launch (start us, length us, event | category | flops | bytes accessed | tf_op | source)
XLA Modules:
  0.0 531.9 jit_solution(3717622361731020790)
XLA Ops:
  6.5 1.2 slice_bitcast_fusion
  7.8 1.4 collective-permute-start
  9.3 3.1 collective-permute-start.1
  12.4 1.3 collective-permute-done.1
  13.7 0.9 select_maximum_fusion.6
  14.6 3.3 fusion.103
  18.1 1.4 collective-permute-start.2
  19.5 3.1 collective-permute-start.3
  22.6 1.3 collective-permute-done.3
  23.9 0.9 select_maximum_fusion.4
  24.8 3.4 fusion.73
  28.3 1.3 collective-permute-start.4
  29.6 3.1 collective-permute-start.5
  32.7 1.3 collective-permute-done.5
  34.0 0.9 select_maximum_fusion.2
  34.9 3.3 fusion.43
  38.3 0.8 fusion.145
  39.2 1.3 collective-permute-start.6
  40.4 3.1 collective-permute-start.7
  43.5 0.7 fusion.150
  46.8 0.7 copy-done.4
  47.6 0.9 select_maximum_fusion
  48.4 4.5 fusion.13
  53.1 1.8 broadcast_select_fusion.3
  55.0 0.7 all-gather.7.cloned.1.call-update
  55.7 0.7 all-gather.9.cloned.1.call-update
  57.0 99.5 %all-gather.5.cloned.1.call-done = bf16[8,2,2,8,48,256]{5,4,3,2,1,0:T(8,128)(2,1)} async-done(((bf16[1,2,2,8,48,256]{5,4,3,2,1,0:T(8,128)(2,1)}), bf16[8,2,2,8,48,256]{5,4,3,2,1,0:T(8,128)(2,1)}) %all-gather.5.cloned.1.call-update) | async-done | bytes 6291472 | tf_op jit(solution)/shard_map/all_gather | solution.py:24
  156.5 3.8 reduce_sum.48
  160.3 95.3 %all-gather.7.cloned.1.call-done = bf16[8,2,2,8,48,256]{5,4,3,2,1,0:T(8,128)(2,1)} async-done(((bf16[1,2,2,8,48,256]{5,4,3,2,1,0:T(8,128)(2,1)}), bf16[8,2,2,8,48,256]{5,4,3,2,1,0:T(8,128)(2,1)}) %all-gather.7.cloned.1.call-update) | async-done | bytes 6291472 | tf_op jit(solution)/shard_map/all_gather | solution.py:24
  255.6 3.8 reduce_sum.49
  259.4 95.3 %all-gather.9.cloned.1.call-done = bf16[8,2,2,8,48,256]{5,4,3,2,1,0:T(8,128)(2,1)} async-done(((bf16[1,2,2,8,48,256]{5,4,3,2,1,0:T(8,128)(2,1)}), bf16[8,2,2,8,48,256]{5,4,3,2,1,0:T(8,128)(2,1)}) %all-gather.9.cloned.1.call-update) | async-done | bytes 6291472 | tf_op jit(solution)/shard_map/all_gather | solution.py:24
  354.7 3.8 reduce_sum.50
  358.5 0.8 fusion.141
  359.3 0.9 fusion.142
  360.2 93.4 %all-gather.11.cloned.1.call-done = bf16[8,2,2,8,48,256]{5,4,3,2,1,0:T(8,128)(2,1)} async-done(((bf16[1,2,2,8,48,256]{5,4,3,2,1,0:T(8,128)(2,1)}), bf16[8,2,2,8,48,256]{5,4,3,2,1,0:T(8,128)(2,1)}) %all-gather.11.cloned.1.call-update) | async-done | bytes 6291472 | tf_op jit(solution)/shard_map/all_gather | solution.py:24
  453.6 3.8 reduce_sum.51
  457.4 0.8 fusion.144
  458.5 0.9 pad.65
  459.8 0.9 pad.66
  461.0 0.9 pad.63
  462.3 0.9 pad.64
  463.6 1.0 pad.61
  464.8 1.0 pad.62
  466.1 0.9 pad.59
  467.4 0.9 pad.60
  468.9 0.9 fusion.135
  470.2 1.0 fusion.133
  471.2 1.4 copy.27
  472.7 2.1 fusion.131
  474.7 2.3 copy.32
  477.0 1.4 copy.15
  478.4 2.4 copy.20
  480.8 2.3 copy.25
  483.2 1.5 copy.30
  484.6 3.3 gather_fusion.1
  487.9 3.3 gather_fusion
  491.2 3.5 gather_fusion.3
  494.7 3.2 gather_fusion.2
  497.9 3.2 gather_fusion.5
  501.1 3.2 gather_fusion.4
  504.3 3.2 gather_fusion.7
  507.5 3.2 gather_fusion.6
  510.7 11.0 %multiply_add_fusion = f32[4,8,48,256]{2,1,3,0:T(8,128)} fusion(bf16[4,8,48,256]{2,1,3,0:T(8,128)(2,1)} %gather_fusion.7, bf16[4,8,48,256]{2,1,3,0:T(8,128)(2,1)} %gather_fusion.6, bf16[4,8,48,256]{2,1,3,0:T(8,128)(2,1)} %gather_fusion.5, bf16[4,8,48,256]{2,1,3,0:T(8,128)(2,1)} %gather_fusion.4, bf16[4,8,48,256]{2,1,3,0:T(8,128)(2,1)} %gather_fusion.3, ...), kind=kLoop, calls=%fused_computation.8 | loop fusion | flops 9043968 | bytes 11010048 | tf_op jit(solution)/shard_map/add | solution.py:64
  521.7 3.7 copy.34
  (63 shorter events, 4.9 us)
Async XLA Ops:
  6.5 5.8 %copy-start.10 = (f32[1,4,8,256]{3,2,1,0:T(8,128)S(1)}, f32[1,4,8,256]{3,2,1,0:T(8,128)}, u32[]{:S(2)}) copy-start(f32[1,4,8,256]{3,2,1,0:T(8,128)} %param.14) | copy-start | bytes 98308
  6.5 150.0 %all-gather.5.cloned.1.call-start = ((), (), s32[]{:S(2)}) async-start(), calls=%async_computation | async-start | bytes 7077888 | tf_op jit(solution)/shard_map/all_gather | solution.py:24
  7.7 6.8 %copy-start = (f32[8,48,256]{2,1,0:T(8,128)S(1)}, f32[8,48,256]{2,1,0:T(8,128)}, u32[]{:S(2)}) copy-start(f32[8,48,256]{2,1,0:T(8,128)} %param.15) | copy-start | bytes 1179652
  7.7 6.8 %copy-start.1 = (f32[1,2,2,8,48,256]{5,4,3,2,1,0:T(8,128)S(1)}, f32[1,2,2,8,48,256]{5,4,3,2,1,0:T(8,128)}, u32[]{:S(2)}) copy-start(f32[1,2,2,8,48,256]{5,4,3,2,1,0:T(8,128)} %param.13) | copy-start | bytes 4718596
  7.8 4.5 collective-permute-start
  9.3 4.4 collective-permute-start.1
  18.0 6.8 %copy-start.2 = (f32[1,2,2,8,48,256]{5,4,3,2,1,0:T(8,128)S(1)}, f32[1,2,2,8,48,256]{5,4,3,2,1,0:T(8,128)}, u32[]{:S(2)}) copy-start(f32[1,2,2,8,48,256]{5,4,3,2,1,0:T(8,128)} %param.13) | copy-start | bytes 4718596
  18.1 4.5 collective-permute-start.2
  19.5 4.4 collective-permute-start.3
  28.3 4.4 collective-permute-start.4
  29.6 4.4 collective-permute-start.5
  34.9 8.6 %copy-start.11 = (s32[4]{0:T(128)S(1)}, s32[4]{0:T(128)}, u32[]{:S(2)}) copy-start(s32[4]{0:T(128)} %param.16) | copy-start | bytes 52
  39.2 7.6 %collective-permute-start.6 = (f32[1,2,4,48,256]{4,3,2,1,0:T(8,128)}, f32[1,2,4,48,256]{4,3,2,1,0:T(8,128)S(1)}, u32[]{:S(2)}, u32[]{:S(2)}) collective-permute-start(f32[1,2,4,48,256]{4,3,2,1,0:T(8,128)} %get-tuple-element.73), channel_id=1, source_target_pairs={{1,0},{3,2},{5,4},{7,6},{9,8},{11,10},{13,12},{15,14},{17,16},{19,... | collective-permute-start | bytes 1179656 | tf_op jit(solution)/shard_map/ppermute | solution.py:17
  40.4 6.4 %collective-permute-start.7 = (f32[1,2,4,48,256]{4,3,2,1,0:T(8,128)S(1)}, f32[1,2,4,48,256]{4,3,2,1,0:T(8,128)S(1)}, u32[]{:S(2)}, u32[]{:S(2)}) collective-permute-start(f32[1,2,4,48,256]{4,3,2,1,0:T(8,128)S(1)} %get-tuple-element.74), channel_id=1, source_target_pairs={{0,1},{2,3},{4,5},{6,7},{8,9},{10,11},{12,13},{14,15},{16,17},{18,... | collective-permute-start | bytes 1179656 | tf_op jit(solution)/shard_map/ppermute | solution.py:16
  46.8 0.7 copy-start.4
  53.1 3.9 copy-start.12
  54.9 200.7 %all-gather.7.cloned.1.call-start = ((), (), s32[]{:S(2)}) async-start(), calls=%async_computation.1 | async-start | bytes 7077888 | tf_op jit(solution)/shard_map/all_gather | solution.py:24
  55.7 299.0 %all-gather.9.cloned.1.call-start = ((), (), s32[]{:S(2)}) async-start(), calls=%async_computation.2 | async-start | bytes 7077888 | tf_op jit(solution)/shard_map/all_gather | solution.py:24
  56.4 397.2 %all-gather.11.cloned.1.call-start = ((), (), s32[]{:S(2)}) async-start(), calls=%async_computation.3 | async-start | bytes 7077888 | tf_op jit(solution)/shard_map/all_gather | solution.py:24
  459.5 3.8 copy-start.9
  460.7 3.8 copy-start.8
  464.5 3.8 copy-start.6
  464.5 3.8 copy-start.7
  466.1 2.8 copy-start.5
  478.4 4.7 copy-start.3
Sparse Core Ops, SparseCore 0:
  55.1 101.3 all-gather.4
  158.7 96.8 all-gather.6
  257.8 96.8 all-gather.8
  356.7 96.8 all-gather.10
